TPU v7x, 256 devices: a whole 4x4x8 slice. The times are simulated.
256 devices in a mesh: dp: 8 (over x, core), tensor: 32 (over y, z).
Axes of the slice: x: 4, y: 4, z: 8, core: 2. Of those that a mesh axis runs over, the one named last changes fastest.
Arguments:
- tokens: bfloat16 [16384, 2048], P(('dp', 'tensor')), may hold values from -6 to 6
- attn_gain: float32 [2048], replicated, may hold values from 0.25 to 1.75
- ffn_gain: float32 [2048], replicated, may hold values from 0.25 to 1.75
- w_attn: bfloat16 [4, 2048, 1024], P(None, None, 'tensor')
- kv_pool: bfloat16 [768, 8, 128, 256], P(('dp', 'tensor'))
- page_table: int32 [8, 72], P('dp'), may hold values from 0 to 95, as said below
- cache_len: int32 [8], P('dp'), may hold values from 2304 to 9216
- routes: int32 [16384, 4], P(('dp', 'tensor')), may hold values from 0 to 63, all different within a row; in each aligned block of 64 rows (0 to 63, 64 to 127, ...) at most 5 rows name the same one
- route_gain: float32 [16384, 4], P(('dp', 'tensor')), may hold values from 0.05 to 0.3
- w_gate_up: bfloat16 [256, 2048, 512], P(('dp', 'tensor')), may hold values from -0.125 to 0.125
- w_down: bfloat16 [256, 256, 2048], P(('dp', 'tensor')), may hold values from -0.1875 to 0.1875
Outputs:
- layer_out: bfloat16 [16384, 2048], P(('dp', 'tensor'))
Inputs may be any that keep to these rules, and one draw needn't show every extreme that they name: `page_table`: each row lists 72 different slots; an entry of value v names slot v % 3 of the device v // 3 along tensor in the request's pool. `routes`: among the 64 tokens of one device no expert is named more than 5 times, and in every draw some expert is named exactly 5 times by one device's tokens. A row names 4 different experts.
All inputs are finite; a program needn't handle non-finite values.
Results may differ from a plain program's by a relative error of at most 0.014.
Values may be sent and summed in bfloat16 or wider, within the bound.
A program may use at most 128 MiB of HBM per device.

v0:
```python
import math
import jax
import jax.numpy as jnp
from jax import lax
from jax.sharding import PartitionSpec as P

HEADS = 8
HD = 128
EXPERTS = 64
TOP = 4
rope_base = 50000.0
norm_eps = 1e-06
very_low = -1e30


def partner(value, axis, apart):
    mask = 2**apart
    pairs = [(source, source ^ mask) for source in range(lax.axis_size(axis))]
    return lax.ppermute(value, axis, pairs)


def rms_scale(rows, gain):
    values = rows.astype(jnp.float32)
    power = jnp.mean(values * values, axis=-1, keepdims=True)
    return (values * lax.rsqrt(power + norm_eps) * gain).astype(jnp.bfloat16)


def rotate(values, positions):
    half = values.shape[-1] // 2
    freq = rope_base ** (-(jnp.arange(half, dtype=jnp.float32) * 2.0) / values.shape[-1])
    angle = positions.astype(jnp.float32)[:, None] * freq[None, :]
    cosine = jnp.cos(angle)
    sine = jnp.sin(angle)
    first = values[:, :half]
    second = values[:, half:]
    return jnp.concatenate([first * cosine - second * sine, second * cosine + first * sine], axis=1)


def expert_pieces(rows, gate_up, down_projected):
    width = down_projected.shape[1]
    both = jnp.einsum("tpacd,pdf->tpacf", rows, gate_up, preferred_element_type=jnp.float32)
    activation = (jax.nn.silu(both[..., :width]) * both[..., width:]).astype(jnp.bfloat16)
    return jnp.einsum(
        "tpacf,pfd->tpacd", activation, down_projected, preferred_element_type=jnp.float32
    )


def local(
    tokens,
    attn_gain,
    ffn_gain,
    w_attn,
    kv_pool,
    page_table,
    cache_len,
    routes,
    route_gain,
    w_gate_up,
    w_down,
):
    tensor_count = lax.axis_size("tensor")
    n_dp = lax.axis_size("dp")
    tok_dev, width = tokens.shape
    split = tensor_count // HEADS
    member = lax.axis_index("tensor")
    head = member // split
    part = member % split
    span = tok_dev * tensor_count
    length = cache_len[0]
    scale = 1.0 / math.sqrt(HD)
    head_cols = w_attn[:3]
    for bit in range(split.bit_length() - 1):
        other = partner(head_cols, "tensor", bit)
        upper = part >> bit & 1 == 1
        head_cols = jnp.where(
            upper,
            jnp.concatenate([other, head_cols], axis=2),
            jnp.concatenate([head_cols, other], axis=2),
        )
    project_w = jnp.concatenate([head_cols[0], head_cols[1], head_cols[2]], axis=1)
    normed = rms_scale(tokens, attn_gain)
    piece = lax.all_gather(normed, "tensor", axis=0, tiled=True)
    positions = length + jnp.arange(piece.shape[0], dtype=jnp.int32)
    product = jnp.dot(piece, project_w, preferred_element_type=jnp.float32)
    query = rotate(product[:, :HD], positions).astype(jnp.bfloat16)
    key_new = rotate(product[:, HD : 2 * HD], positions).astype(jnp.bfloat16)
    mixed = jnp.concatenate([query, key_new, product[:, 2 * HD :].astype(jnp.bfloat16)], axis=1)
    query = mixed[:, :HD]
    new_rows = span // split
    own_new = lax.dynamic_slice_in_dim(mixed, part * new_rows, new_rows, 0)
    slots = kv_pool.shape[0]
    page = kv_pool.shape[2]
    sub = page // split
    sent = kv_pool.reshape(slots, HEADS * split, sub, 2 * HD)
    arrived = lax.all_to_all(sent, "tensor", split_axis=1, concat_axis=0, tiled=True)
    cached = arrived.reshape(tensor_count * slots * sub, 2 * HD)
    table = page_table[0]
    slot_ids = jnp.arange(tensor_count * slots, dtype=jnp.int32)
    hits = table[None, :] == slot_ids[:, None]
    page_of = jnp.sum(
        jnp.where(hits, jnp.arange(table.shape[0], dtype=jnp.int32)[None, :], 0), axis=1
    )
    present = jnp.any(hits, axis=1)
    position = page_of[:, None] * page + part * sub + jnp.arange(sub, dtype=jnp.int32)[None, :]
    live = (present[:, None] & (position < length)).reshape(-1)
    live_all = jnp.concatenate([live, jnp.ones((new_rows,), dtype=bool)])
    keys = jnp.concatenate([cached[:, :HD], own_new[:, HD : 2 * HD]], axis=0)
    values = jnp.concatenate([cached[:, HD:], own_new[:, 2 * HD :]], axis=0)
    q_block = math.gcd(span, 512)
    q_count = span // q_block
    query_blocks = query.reshape(q_count, q_block, HD)

    def block_scores(rows):
        scores = (
            lax.dot_general(
                rows, keys, (((1,), (1,)), ((), ())), preferred_element_type=jnp.float32
            )
            * scale
        )
        return jnp.where(live_all[None, :], scores, very_low)

    column = jnp.arange(HEADS, dtype=jnp.int32)[None, :] == head

    def local_max(rows):
        return jnp.max(block_scores(rows), axis=1)

    local_top = lax.map(local_max, query_blocks).reshape(span)
    top_cols = lax.pmax(
        jnp.where(column, local_top[:, None], very_low).astype(jnp.bfloat16), "tensor"
    ).astype(jnp.float32)
    row_top = jnp.sum(jnp.where(column, top_cols, 0.0), axis=1)

    def weigh_sum(inputs):
        rows, top = inputs
        expo = jnp.exp(block_scores(rows) - top[:, None])
        return (
            jnp.dot(expo.astype(jnp.bfloat16), values, preferred_element_type=jnp.float32),
            jnp.sum(expo, axis=1),
        )

    weighted, sums = lax.map(weigh_sum, (query_blocks, row_top.reshape(q_count, q_block)))
    weighted = weighted.reshape(span, HD)
    total_cols = lax.psum(
        jnp.where(column, sums.reshape(span)[:, None], 0.0).astype(jnp.bfloat16), "tensor"
    ).astype(jnp.float32)
    own_totals = lax.dynamic_slice_in_dim(total_cols, member * tok_dev, tok_dev, 0)
    landed_rows = lax.all_to_all(
        weighted.reshape(span, 1, HD).astype(jnp.bfloat16),
        "tensor",
        split_axis=0,
        concat_axis=1,
        tiled=True,
    ).astype(jnp.float32)
    numer = jnp.sum(landed_rows.reshape(tok_dev, HEADS, split, HD), axis=2)
    merged = (numer / own_totals[..., None]).reshape(tok_dev, HEADS * HD)
    attn = jnp.zeros((tok_dev, width), jnp.float32) + lax.dot_general(
        merged,
        lax.all_gather(w_attn[3], "tensor", axis=1, tiled=True).astype(jnp.float32),
        (((1,), (1,)), ((), ())),
        precision=lax.Precision.HIGHEST,
    )
    hidden = (tokens.astype(jnp.float32) + attn).astype(jnp.bfloat16)
    normed2 = rms_scale(hidden, ffn_gain)
    per_dev = w_gate_up.shape[0]
    exp_dp = EXPERTS // n_dp
    exp_t = exp_dp // per_dev
    quarters = tensor_count // exp_t
    cap = routes.shape[0] * 0 + max(2, tok_dev * TOP * 5 // (4 * EXPERTS))
    flat_expert = routes.reshape(-1)
    onehot = (flat_expert[:, None] == jnp.arange(EXPERTS, dtype=jnp.int32)[None, :]).astype(
        jnp.int32
    )
    rank = jnp.sum(jnp.cumsum(onehot, axis=0) * onehot, axis=1) - 1
    slot_id = (flat_expert % exp_dp * n_dp + flat_expert // exp_dp) * cap + rank
    total_slots = exp_dp * n_dp * cap
    place = (slot_id[:, None] == jnp.arange(total_slots, dtype=jnp.int32)[None, :]).astype(
        jnp.float32
    )
    token_of = (
        jnp.arange(tok_dev * TOP, dtype=jnp.int32)[:, None] // TOP
        == jnp.arange(tok_dev, dtype=jnp.int32)[None, :]
    ).astype(jnp.float32)
    dispatch = jnp.dot(place.T, token_of, precision=lax.Precision.HIGHEST).astype(jnp.bfloat16)
    combine = jnp.dot(
        token_of.T, place * route_gain.reshape(-1)[:, None], precision=lax.Precision.HIGHEST
    )
    buffer = jnp.dot(dispatch, normed2, preferred_element_type=jnp.float32).astype(jnp.bfloat16)
    buffer = buffer.reshape(exp_dp, n_dp, cap, width)
    landed = lax.all_to_all(buffer, "dp", split_axis=1, concat_axis=1, tiled=True)
    grouped = landed.reshape(exp_t, per_dev, n_dp, cap, width)
    copies = jnp.broadcast_to(grouped[None], (quarters, exp_t, per_dev, n_dp, cap, width)).reshape(
        tensor_count, per_dev, n_dp, cap, width
    )
    partial_out = expert_pieces(
        lax.all_to_all(copies, "tensor", split_axis=0, concat_axis=0, tiled=True), w_gate_up, w_down
    ).astype(jnp.bfloat16)
    returned = lax.all_to_all(partial_out, "tensor", split_axis=0, concat_axis=0, tiled=True)
    summed = jnp.sum(
        returned.astype(jnp.float32).reshape(quarters, exp_dp, n_dp, cap, width), axis=0
    )
    output_rows = lax.all_to_all(
        summed.astype(jnp.bfloat16), "dp", split_axis=1, concat_axis=1, tiled=True
    ).astype(summed.dtype)
    moe = jnp.dot(combine, output_rows.reshape(total_slots, width), precision=lax.Precision.HIGHEST)
    return (hidden.astype(jnp.float32) + moe).astype(jnp.bfloat16)


def solution(mesh):
    placed = (
        P(("dp", "tensor"), None),
        P(),
        P(),
        P(None, None, "tensor"),
        P(("dp", "tensor"), None, None, None),
        P("dp", None),
        P("dp"),
        P(("dp", "tensor"), None),
        P(("dp", "tensor"), None),
        P(("dp", "tensor"), None, None),
        P(("dp", "tensor"), None, None),
    )
    return jax.shard_map(
        local, mesh=mesh, in_specs=placed, out_specs=P(("dp", "tensor"), None), check_vma=False
    )
```

profile of v0, /device:TPU:1, one launch (start us, length us, event | category | flops | bytes accessed | tf_op | source)
XLA Modules:
  0.0 833.4 jit_solution(3819508705786121760)
XLA Ops:
  9.6 2.7 copy.60
  12.3 12.3 %all-to-all-start = ((bf16[3,32,32,256]{3,2,0,1:T(8,128)(2,1)}), bf16[3,32,32,256]{3,2,0,1:T(8,128)(2,1)}, u32[]{:S(2)}, u32[]{:S(2)}) async-start(bf16[3,32,32,256]{3,2,0,1:T(8,128)(2,1)} %copy.60), calls=%async_computation | async-start | bytes 3145728 | tf_op jit(solution)/shard_map/all_to_all | solution.py:95
  28.0 50.1 %collective-permute-done = bf16[3,2048,32]{1,2,0:T(8,128)(2,1)} collective-permute-done((bf16[3,2048,32]{1,2,0:T(8,128)(2,1)S(1)}, bf16[3,2048,32]{1,2,0:T(8,128)(2,1)}, u32[]{:S(2)}, u32[]{:S(2)}) %collective-permute-start) | collective-permute-done | bytes 393248 | tf_op jit(solution)/shard_map/ppermute | solution.py:19
  83.1 49.2 %collective-permute-done.1 = bf16[3,2048,64]{1,2,0:T(8,128)(2,1)} collective-permute-done((bf16[3,2048,64]{1,2,0:T(8,128)(2,1)S(1)}, bf16[3,2048,64]{1,2,0:T(8,128)(2,1)}, u32[]{:S(2)}, u32[]{:S(2)}) %collective-permute-start.1) | collective-permute-done | bytes 786464 | tf_op jit(solution)/shard_map/ppermute | solution.py:19
  137.8 16.5 %all-gather.4.cloned.1.call-done = bf16[2048,2048]{1,0:T(8,128)(2,1)} async-done(((bf16[64,2048]{1,0:T(8,128)(2,1)}), bf16[2048,2048]{1,0:T(8,128)(2,1)}) %all-gather.4.cloned.1.call-update) | async-done | bytes 8388624 | tf_op jit(solution)/shard_map/all_gather | solution.py:82
  154.3 6.1 fusion.34
  160.5 2.9 constant_dynamic-update-slice_fusion.1
  163.4 2.9 constant_dynamic-update-slice_fusion
  178.1 10.1 %while.22 = (s32[]{:T(128)}, bf16[4,512]{1,0:T(4,128)(2,1)S(1)}, pred[3584]{0:T(1024)(128)(4,1)S(1)}, bf16[4,512,128]{2,1,0:T(8,128)(2,1)}, bf16[3584,128]{1,0:T(8,128)(2,1)}, /*index=5*/s32[]{:T(128)}, s32[]{:T(128)}) while((s32[]{:T(128)}, bf16[4,512]{1,0:T(4,128)(2,1)S(1)}, pred[3584]{0:T(1024)(128)(4,1)S(1)}, ...), condition=%wide.region_5.6_spmd, body=%wide.region_3.5_spmd.sunk | while | flops 475266560 | bytes 1058897 | solution.py:127
  188.3 115.9 %pmax.7 = bf16[2048,8]{0,1:T(8,128)(2,1)S(1)} all-reduce(bf16[2048,8]{0,1:T(8,128)(2,1)S(1)} %select_convert_fusion.1), channel_id=1, replica_groups=mesh['dp'=8,'tensor'=32] {'tensor'}, use_global_device_ids=true, to_apply=%region_6.7 | all-reduce | flops 16384 | bytes 65536 | tf_op jit(solution)/shard_map/pmax | solution.py:128
  305.6 21.5 %while.23 = (s32[]{:T(128)}, bf16[4,512,128]{2,1,0:T(8,128)(2,1)}, bf16[4,512]{1,0:T(4,128)(2,1)S(1)}, pred[3584]{0:T(1024)(128)(4,1)}, bf16[4,512,128]{2,1,0:T(...) while((s32[]{:T(128)}, bf16[4,512,128]{2,1,0:T(8,128)(2,1)}, ...), condition=%wide.region_10.11_spmd, body=%wide.region_8.10_spmd.sunk | while | flops 948698624 | bytes 13779625 | solution.py:141
  305.6 3.3 fusion.113
  311.0 3.3 fusion.113
  316.3 3.4 fusion.113
  321.7 3.3 fusion.113
  330.5 3.9 all-to-all-start.1
  334.9 115.8 %psum.7 = bf16[2048,8]{0,1:T(8,128)(2,1)S(1)} all-reduce(bf16[2048,8]{0,1:T(8,128)(2,1)S(1)} %select_convert_fusion), channel_id=1, replica_groups=mesh['dp'=8,'tensor'=32] {'tensor'}, use_global_device_ids=true, to_apply=%region_12.13 | all-reduce | flops 16384 | bytes 65536 | tf_op jit(solution)/shard_map/psum | solution.py:143
  455.5 4.8 multiply_reduce_fusion
  465.8 77.6 %all_to_all.44 = bf16[8,8,5,2048]{3,0,2,1:T(8,128)(2,1)S(1)} all-to-all(bf16[8,8,5,2048]{3,0,2,1:T(8,128)(2,1)S(1)} %copy.69), channel_id=1, replica_groups=mesh['dp'=8,'tensor'=32] {'dp'}, dimensions={1} | all-to-all | bytes 2621440 | tf_op jit(solution)/shard_map/all_to_all | solution.py:189
  544.8 117.5 %all_to_all.45 = bf16[32,1,8,5,2048]{4,2,3,1,0:T(8,128)(2,1)S(1)} all-to-all(bf16[32,1,8,5,2048]{4,2,3,1,0:T(8,128)(2,1)S(1)} %bitcast.148), channel_id=1, replica_groups=mesh['dp'=8,'tensor'=32] {'tensor'}, dimensions={0} | all-to-all | bytes 10485760 | tf_op jit(solution)/shard_map/all_to_all | solution.py:195
  662.4 2.9 fusion.29
  666.8 123.0 %all_to_all.46 = bf16[32,1,8,5,2048]{4,2,3,1,0:T(8,128)(2,1)S(1)} all-to-all(bf16[32,1,8,5,2048]{4,2,3,1,0:T(8,128)(2,1)S(1)} %convert_bitcast_fusion), channel_id=1, replica_groups=mesh['dp'=8,'tensor'=32] {'tensor'}, dimensions={0} | all-to-all | bytes 10485760 | tf_op jit(solution)/shard_map/all_to_all | solution.py:197
  792.6 8.6 %all-to-all-start.5 = ((bf16[8,8,5,2048]{3,0,2,1:T(8,128)(2,1)}), bf16[8,8,5,2048]{3,0,2,1:T(8,128)(2,1)S(1)}, u32[]{:S(2)}, u32[]{:S(2)}) async-start(bf16[8,8,5,2048]{3,0,2,1:T(8,128)(2,1)} %copy.72), calls=%async_computation.5 | async-start | bytes 2621440 | tf_op jit(solution)/shard_map/all_to_all | solution.py:201
  801.9 17.3 %all-to-all-done.5 = bf16[8,8,5,2048]{3,0,2,1:T(8,128)(2,1)S(1)} async-done(((bf16[8,8,5,2048]{3,0,2,1:T(8,128)(2,1)}), bf16[8,8,5,2048]{3,0,2,1:T(8,128)(2,1)S(1)}, u32[]{:S(2)}, u32[]{:S(2)}) %all-to-all-start.5) | async-done | bytes 1310752 | tf_op jit(solution)/shard_map/all_to_all | solution.py:201
  (148 shorter events, 75.3 us)
Async XLA Ops:
  6.5 655.8 %copy-start = (bf16[1,2048,512]{2,1,0:T(8,128)(2,1)S(1)}, bf16[1,2048,512]{2,1,0:T(8,128)(2,1)}, u32[]{:S(2)}) copy-start(bf16[1,2048,512]{2,1,0:T(8,128)(2,1)} %param.24) | copy-start | bytes 6291460
  6.5 147.8 %all-gather.4.cloned.1.call-start = ((), (), s32[]{:S(2)}) async-start(), calls=%async_computation.6 | async-start | bytes 8650752 | tf_op jit(solution)/shard_map/all_gather | solution.py:82
  12.3 12.3 %copy-start.4 = (bf16[4,2048,32]{1,2,0:T(8,128)(2,1)S(1)}, bf16[4,2048,32]{1,2,0:T(8,128)(2,1)}, u32[]{:S(2)}) copy-start(bf16[4,2048,32]{1,2,0:T(8,128)(2,1)} %param.18) | copy-start | bytes 1572868
  12.3 14.3 %copy-start.17 = (s32[1,72]{1,0:T(1,128)S(1)}, s32[1,72]{1,0:T(1,128)}, u32[]{:S(2)}) copy-start(s32[1,72]{1,0:T(1,128)} %param.20) | copy-start | bytes 868
  12.3 14.5 %copy-start.14 = (s32[64,4]{0,1:T(4,128)S(1)}, s32[64,4]{0,1:T(4,128)}, u32[]{:S(2)}) copy-start(s32[64,4]{0,1:T(4,128)} %param.22) | copy-start | bytes 3076
  12.3 123.2 %all-to-all-start = ((bf16[3,32,32,256]{3,2,0,1:T(8,128)(2,1)}), bf16[3,32,32,256]{3,2,0,1:T(8,128)(2,1)}, u32[]{:S(2)}, u32[]{:S(2)}) async-start(bf16[3,32,32,256]{3,2,0,1:T(8,128)(2,1)} %copy.60), calls=%async_computation | async-start | bytes 3145728 | tf_op jit(solution)/shard_map/all_to_all | solution.py:95
  24.6 431.0 %all-gather.6.cloned.1.call-start = ((), (), s32[]{:S(2)}) async-start(), calls=%async_computation.7 | async-start | bytes 4325376 | tf_op jit(solution)/shard_map/all_gather | solution.py:158
  24.7 53.4 %collective-permute-start = (bf16[3,2048,32]{1,2,0:T(8,128)(2,1)S(1)}, bf16[3,2048,32]{1,2,0:T(8,128)(2,1)}, u32[]{:S(2)}, u32[]{:S(2)}) collective-permute-start(bf16[3,2048,32]{1,2,0:T(8,128)(2,1)S(1)} %slice.61), channel_id=1, source_target_pairs={{0,1},{1,0},{2,3},{3,2},{4,5},{5,4},{6,7},{7,6},{8,9},{9,8},{10,11... | collective-permute-start | bytes 1179656 | tf_op jit(solution)/shard_map/ppermute | solution.py:19
  27.1 105.2 %copy-start.7 = (s32[256]{0:T(256)}, s32[256]{0:T(256)S(1)}, u32[]{:S(2)}) copy-start(s32[256]{0:T(256)S(1)} %reshape.245) | copy-start | bytes 3076
  79.6 52.7 %collective-permute-start.1 = (bf16[3,2048,64]{1,2,0:T(8,128)(2,1)S(1)}, bf16[3,2048,64]{1,2,0:T(8,128)(2,1)}, u32[]{:S(2)}, u32[]{:S(2)}) collective-permute-start(bf16[3,2048,64]{1,2,0:T(8,128)(2,1)S(1)} %maximum_select_fusion.1), channel_id=1, source_target_pairs={{0,2},{1,3},{2,0},{3,1},{4,6},{5,7},{6,4},{7,5},{8,10},{9,11},{10,... | collective-permute-start | bytes 2359304 | tf_op jit(solution)/shard_map/ppermute | solution.py:19
  82.4 221.8 %copy-start.10 = (pred[8]{0:T(512)(128)(4,1)}, pred[8]{0:T(512)(128)(4,1)S(1)}, u32[]{:S(2)}) copy-start(pred[8]{0:T(512)(128)(4,1)S(1)} %iota_compare_fusion.9) | copy-start | bytes 28
  178.1 126.2 %copy-start.3 = (bf16[512,128]{0,1:T(8,128)(2,1)S(1)}, bf16[512,128]{0,1:T(8,128)(2,1)}, u32[]{:S(2)}) copy-start(bf16[512,128]{0,1:T(8,128)(2,1)} %get-tuple-element.112) | copy-start | bytes 393220
  188.2 116.0 %copy-start.13 = (pred[3584]{0:T(1024)(128)(4,1)}, pred[3584]{0:T(1024)(128)(4,1)S(1)}, u32[]{:S(2)}) copy-start(pred[3584]{0:T(1024)(128)(4,1)S(1)} %get-tuple-element.275) | copy-start | bytes 10756
  305.6 3.4 copy-start.5
  311.0 3.3 copy-start.5
  316.3 3.4 copy-start.5
  321.7 3.3 copy-start.5
  327.0 7.4 copy-start.8
  327.1 7.4 copy-start.12
  327.1 7.7 copy-start.11
  330.5 120.2 %all-to-all-start.1 = ((bf16[32,2,4096]{2,1,0:T(2,128)(2,1)}), bf16[32,2,4096]{2,1,0:T(2,128)(2,1)S(1)}, u32[]{:S(2)}, u32[]{:S(2)}) async-start(bf16[32,2,4096]{2,1,0:T(2,128)(2,1)} %reshape.261), calls=%async_computation.1 | async-start | bytes 1048576 | tf_op jit(solution)/shard_map/all_to_all | solution.py:147
  455.5 5.6 copy-start.9
  792.6 8.7 %copy-start.15 = (f32[64,4]{0,1:T(4,128)S(1)}, f32[64,4]{0,1:T(4,128)}, u32[]{:S(2)}) copy-start(f32[64,4]{0,1:T(4,128)} %param.23) | copy-start | bytes 3076
  792.6 26.6 %all-to-all-start.5 = ((bf16[8,8,5,2048]{3,0,2,1:T(8,128)(2,1)}), bf16[8,8,5,2048]{3,0,2,1:T(8,128)(2,1)S(1)}, u32[]{:S(2)}, u32[]{:S(2)}) async-start(bf16[8,8,5,2048]{3,0,2,1:T(8,128)(2,1)} %copy.72), calls=%async_computation.5 | async-start | bytes 2621440 | tf_op jit(solution)/shard_map/all_to_all | solution.py:201
  (7 other events, 10.0 us)
Sparse Core Ops, SparseCore 0:
  10.0 144.3 all-gather.3
  156.9 81.2 all-gather.5
where the time goes:
time: 835 us; the launch traced here: 833 us
  blocking collectives  550 us (66%)
  waiting for transfers between devices  133 us (16%)
  matrix products  47.3 us (6%)
  local copies, waits for them, and re-layouts  31.3 us (4%)
  other arithmetic  29.2 us (3%)
  starting transfers between devices  28 us (3%)
  between operations  14.5 us (2%)
    all_to_all x1, blocking collectives, local(): lax.all_to_all(partial_out, 'tensor', split_axis=0, concat_axis=0, tiled=...  123 us
    all_to_all x1, blocking collectives, local(): lax.all_to_all(copies, 'tensor', split_axis=0, concat_axis=0, tiled=True)  118 us
    pmax x1, blocking collectives, local(): lax.pmax(jnp.where(column, local_top[:, None], very_low).astype(jnp.bfloa...  116 us
    psum x1, blocking collectives, local(): lax.psum(jnp.where(column, sums.reshape(span)[:, None], 0.0).astype(jnp.b...  116 us
    ppermute x2, waiting for transfers between devices, partner(): return lax.ppermute(value, axis, pairs)  99.3 us
    all_to_all x1, blocking collectives, local(): lax.all_to_all(buffer, 'dp', split_axis=1, concat_axis=1, tiled=True)  77.6 us
    dot_general x8, matrix products, block_scores(): lax.dot_general(rows, keys, (((1,), (1,)), ((), ())), preferred_element_t...  23.3 us
    all_to_all x1, waiting for transfers between devices, local(): lax.all_to_all(summed.astype(jnp.bfloat16), 'dp', split_axis=1, concat_ax...  17.3 us
  transfers between devices with their start and end apart: 7, of which 4 were waited for; matrix products, arithmetic and copies ran while one was open for 9% of the time, Pallas kernels for 0%

commit v1 on v0

--- a/solution.py
+++ b/solution.py
@@ -11,6 +11,22 @@
 rope_base = 50000.0
 norm_eps = 1e-06
 very_low = -1e30
+
+
+def swapped_with_each(value, axis, split, join):
+    ways, here = (lax.axis_size(axis), lax.axis_index(axis))
+    width = value.shape[split] // ways
+    shape = list(value.shape)
+    shape[split] = width
+    height = shape[join]
+    shape[join] = height * ways
+    full = jnp.zeros(shape, value.dtype)
+    for mask in range(ways):
+        part = lax.dynamic_slice_in_dim(value, (here ^ mask) * width, width, axis=split)
+        if mask:
+            part = lax.ppermute(part, axis, [(d, d ^ mask) for d in range(ways)])
+        full = lax.dynamic_update_slice_in_dim(full, part, (here ^ mask) * height, axis=join)
+    return full
 
 
 def partner(value, axis, apart):
@@ -186,7 +202,7 @@
     )
     buffer = jnp.dot(dispatch, normed2, preferred_element_type=jnp.float32).astype(jnp.bfloat16)
     buffer = buffer.reshape(exp_dp, n_dp, cap, width)
-    landed = lax.all_to_all(buffer, "dp", split_axis=1, concat_axis=1, tiled=True)
+    landed = swapped_with_each(buffer, "dp", 1, 1)
     grouped = landed.reshape(exp_t, per_dev, n_dp, cap, width)
     copies = jnp.broadcast_to(grouped[None], (quarters, exp_t, per_dev, n_dp, cap, width)).reshape(
         tensor_count, per_dev, n_dp, cap, width

time: 835 us -> 854 us (1.023)
  blocking collectives: 550 us -> 473 us
  starting transfers between devices: 28 us -> 95.1 us
  waiting for transfers between devices: 133 us -> 151 us
  local copies, waits for them, and re-layouts: 31.3 us -> 42.6 us
    all_to_all x1 -> x0, blocking collectives: 77.6 us -> none  [local(): lax.all_to_all(buffer, 'dp', split_axis=1, concat_axis=1, tiled=True)]
    ppermute x0 -> x7, starting transfers between devices: none -> 66.7 us  [swapped_with_each(): part = lax.ppermute(part, axis, [(d, d ^ mask) for d in range(ways)])]
    ppermute x0 -> x7, waiting for transfers between devices: none -> 19 us  [swapped_with_each(): part = lax.ppermute(part, axis, [(d, d ^ mask) for d in range(ways)])]
    dynamic_update_slice x0 -> x8, local copies, waits for them, and re-layouts: none -> 11.8 us  [swapped_with_each(): lax.dynamic_update_slice_in_dim(full, part, (here ^ mask) * height, axis=...]
  transfers between devices with their start and end apart: 7 -> 14, of which waited for: 4 -> 9; matrix products, arithmetic and copies ran while one was open for 9% -> 9% of each run, Pallas kernels for 0% -> 0%
where the time goes in v1:
time: 854 us; the launch traced here: 853 us
  blocking collectives  473 us (55%)
  waiting for transfers between devices  151 us (18%)
  starting transfers between devices  95.1 us (11%)
  matrix products  47.2 us (6%)
  local copies, waits for them, and re-layouts  42.6 us (5%)
  other arithmetic  29.2 us (3%)
  between operations  14.6 us (2%)
    all_to_all x1, blocking collectives, local(): lax.all_to_all(partial_out, 'tensor', split_axis=0, concat_axis=0, tiled=...  122 us
    all_to_all x1, blocking collectives, local(): lax.all_to_all(copies, 'tensor', split_axis=0, concat_axis=0, tiled=True)  119 us
    psum x1, blocking collectives, local(): lax.psum(jnp.where(column, sums.reshape(span)[:, None], 0.0).astype(jnp.b...  116 us
    pmax x1, blocking collectives, local(): lax.pmax(jnp.where(column, local_top[:, None], very_low).astype(jnp.bfloa...  115 us
    ppermute x2, waiting for transfers between devices, partner(): return lax.ppermute(value, axis, pairs)  99.9 us
    ppermute x7, starting transfers between devices, swapped_with_each(): part = lax.ppermute(part, axis, [(d, d ^ mask) for d in range(ways)])  66.7 us
    dot_general x8, matrix products, block_scores(): lax.dot_general(rows, keys, (((1,), (1,)), ((), ())), preferred_element_t...  23.2 us
    ppermute x7, waiting for transfers between devices, swapped_with_each(): part = lax.ppermute(part, axis, [(d, d ^ mask) for d in range(ways)])  19 us
  transfers between devices with their start and end apart: 14, of which 9 were waited for; matrix products, arithmetic and copies ran while one was open for 9% of the time, Pallas kernels for 0%

profile of v1, /device:TPU:1, one launch (start us, length us, event | category | flops | bytes accessed | tf_op | source)
XLA Modules:
  0.0 852.5 jit_solution(18431242166305155921)
XLA Ops:
  12.3 12.3 %all-to-all-start = ((bf16[3,32,32,256]{3,2,0,1:T(8,128)(2,1)}), bf16[3,32,32,256]{3,2,0,1:T(8,128)(2,1)}, u32[]{:S(2)}, u32[]{:S(2)}) async-start(bf16[3,32,32,256]{3,2,0,1:T(8,128)(2,1)} %copy.62), calls=%async_computation | async-start | bytes 3145728 | tf_op jit(solution)/shard_map/all_to_all | solution.py:111
  28.1 50.0 %collective-permute-done = bf16[3,2048,32]{1,2,0:T(8,128)(2,1)} collective-permute-done((bf16[3,2048,32]{1,2,0:T(8,128)(2,1)S(1)}, bf16[3,2048,32]{1,2,0:T(8,128)(2,1)}, u32[]{:S(2)}, u32[]{:S(2)}) %collective-permute-start) | collective-permute-done | bytes 393248 | tf_op jit(solution)/shard_map/ppermute | solution.py:35
  83.2 49.8 %collective-permute-done.1 = bf16[3,2048,64]{1,2,0:T(8,128)(2,1)} collective-permute-done((bf16[3,2048,64]{1,2,0:T(8,128)(2,1)S(1)}, bf16[3,2048,64]{1,2,0:T(8,128)(2,1)}, u32[]{:S(2)}, u32[]{:S(2)}) %collective-permute-start.1) | collective-permute-done | bytes 786464 | tf_op jit(solution)/shard_map/ppermute | solution.py:35
  138.6 14.9 %all-gather.4.cloned.1.call-done = bf16[2048,2048]{1,0:T(8,128)(2,1)} async-done(((bf16[64,2048]{1,0:T(8,128)(2,1)}), bf16[2048,2048]{1,0:T(8,128)(2,1)}) %all-gather.4.cloned.1.call-update) | async-done | bytes 8388624 | tf_op jit(solution)/shard_map/all_gather | solution.py:98
  153.5 6.1 fusion.34
  177.2 10.1 %while.22 = (s32[]{:T(128)}, bf16[4,512]{1,0:T(4,128)(2,1)S(1)}, pred[3584]{0:T(1024)(128)(4,1)S(1)}, bf16[4,512,128]{2,1,0:T(8,128)(2,1)}, bf16[3584,128]{1,0:T(8,128)(2,1)}, /*index=5*/s32[]{:T(128)}, s32[]{:T(128)}) while((s32[]{:T(128)}, bf16[4,512]{1,0:T(4,128)(2,1)S(1)}, pred[3584]{0:T(1024)(128)(4,1)S(1)}, ...), condition=%wide.region_5.6_spmd, body=%wide.region_3.5_spmd.sunk | while | flops 475266560 | bytes 1058897 | solution.py:143
  187.3 115.5 %pmax.7 = bf16[2048,8]{0,1:T(8,128)(2,1)S(1)} all-reduce(bf16[2048,8]{0,1:T(8,128)(2,1)S(1)} %select_convert_fusion.1), channel_id=1, replica_groups=mesh['dp'=8,'tensor'=32] {'tensor'}, use_global_device_ids=true, to_apply=%region_6.7 | all-reduce | flops 16384 | bytes 65536 | tf_op jit(solution)/shard_map/pmax | solution.py:144
  304.3 21.4 %while.23 = (s32[]{:T(128)}, bf16[4,512,128]{2,1,0:T(8,128)(2,1)}, bf16[4,512]{1,0:T(4,128)(2,1)S(1)}, pred[3584]{0:T(1024)(128)(4,1)}, bf16[4,512,128]{2,1,0:T(...) while((s32[]{:T(128)}, bf16[4,512,128]{2,1,0:T(8,128)(2,1)}, ...), condition=%wide.region_10.11_spmd, body=%wide.region_8.10_spmd.sunk | while | flops 948698624 | bytes 13779625 | solution.py:157
  304.3 3.3 fusion.114
  309.6 3.3 fusion.114
  315.0 3.3 fusion.114
  320.3 3.3 fusion.114
  329.2 3.9 all-to-all-start.1
  333.5 116.3 %psum.7 = bf16[2048,8]{0,1:T(8,128)(2,1)S(1)} all-reduce(bf16[2048,8]{0,1:T(8,128)(2,1)S(1)} %select_convert_fusion), channel_id=1, replica_groups=mesh['dp'=8,'tensor'=32] {'tensor'}, use_global_device_ids=true, to_apply=%region_12.13 | all-reduce | flops 16384 | bytes 65536 | tf_op jit(solution)/shard_map/psum | solution.py:159
  454.6 4.8 multiply_reduce_fusion
  464.2 55.7 %collective-permute-start.2 = (bf16[8,1,5,2048]{3,2,1,0:T(8,128)(2,1)S(1)}, bf16[8,1,5,2048]{3,2,1,0:T(8,128)(2,1)S(1)}, u32[]{:S(2)}, u32[]{:S(2)}) collective-permute-start(bf16[8,1,5,2048]{3,2,1,0:T(8,128)(2,1)S(1)} %get-tuple-element.116), channel_id=1, source_target_pairs={{0,32},{32,0},{64,96},{96,64},{128,160},{160,128},{192,224},{224,1... | collective-permute-start | bytes 491528 | tf_op jit(solution)/shard_map/ppermute | solution.py:27
  527.8 3.6 collective-permute-start.8
  534.4 6.8 collective-permute-done.5
  541.2 5.8 collective-permute-done.6
  552.0 10.7 %dynamic_update_slice.66 = bf16[8,8,5,2048]{3,1,2,0:T(8,128)(2,1)S(1)} dynamic-update-slice(bf16[8,8,5,2048]{3,1,2,0:T(8,128)(2,1)S(1)} %copy.71, bf16[8,1,5,2048]{3,1,2,0:T(2,128)(2,1)} %copy.72, s32[]{:T(128)} %constant.153.clone.1, s32[]{:T(128)S(6)} %select_n.140, s32[]{:T(128)} %constant.153.clone.1, s32[]{:T(128)} %constant.153.clone.1) | dynamic-update-slice | bytes 327684 | tf_op jit(solution)/shard_map/dynamic_update_slice | solution.py:28
  563.4 118.8 %all_to_all.39 = bf16[32,1,8,5,2048]{4,2,3,1,0:T(8,128)(2,1)S(1)} all-to-all(bf16[32,1,8,5,2048]{4,2,3,1,0:T(8,128)(2,1)S(1)} %bitcast.148), channel_id=1, replica_groups=mesh['dp'=8,'tensor'=32] {'tensor'}, dimensions={0} | all-to-all | bytes 10485760 | tf_op jit(solution)/shard_map/all_to_all | solution.py:211
  686.7 122.1 %all_to_all.40 = bf16[32,1,8,5,2048]{4,2,3,1,0:T(8,128)(2,1)S(1)} all-to-all(bf16[32,1,8,5,2048]{4,2,3,1,0:T(8,128)(2,1)S(1)} %convert_bitcast_fusion), channel_id=1, replica_groups=mesh['dp'=8,'tensor'=32] {'tensor'}, dimensions={0} | all-to-all | bytes 10485760 | tf_op jit(solution)/shard_map/all_to_all | solution.py:213
  811.5 9.0 %all-to-all-start.4 = ((bf16[8,8,5,2048]{3,0,2,1:T(8,128)(2,1)}), bf16[8,8,5,2048]{3,0,2,1:T(8,128)(2,1)S(1)}, u32[]{:S(2)}, u32[]{:S(2)}) async-start(bf16[8,8,5,2048]{3,0,2,1:T(8,128)(2,1)} %copy.74), calls=%async_computation.4 | async-start | bytes 2621440 | tf_op jit(solution)/shard_map/all_to_all | solution.py:217
  821.1 17.3 %all-to-all-done.4 = bf16[8,8,5,2048]{3,0,2,1:T(8,128)(2,1)S(1)} async-done(((bf16[8,8,5,2048]{3,0,2,1:T(8,128)(2,1)}), bf16[8,8,5,2048]{3,0,2,1:T(8,128)(2,1)S(1)}, u32[]{:S(2)}, u32[]{:S(2)}) %all-to-all-start.4) | async-done | bytes 1310752 | tf_op jit(solution)/shard_map/all_to_all | solution.py:217
  (172 shorter events, 101.0 us)
Async XLA Ops:
  6.5 675.6 %copy-start = (bf16[1,2048,512]{2,1,0:T(8,128)(2,1)S(1)}, bf16[1,2048,512]{2,1,0:T(8,128)(2,1)}, u32[]{:S(2)}) copy-start(bf16[1,2048,512]{2,1,0:T(8,128)(2,1)} %param.24) | copy-start | bytes 6291460
  6.5 146.9 %all-gather.4.cloned.1.call-start = ((), (), s32[]{:S(2)}) async-start(), calls=%async_computation.5 | async-start | bytes 8650752 | tf_op jit(solution)/shard_map/all_gather | solution.py:98
  12.3 12.3 %copy-start.5 = (bf16[4,2048,32]{1,2,0:T(8,128)(2,1)S(1)}, bf16[4,2048,32]{1,2,0:T(8,128)(2,1)}, u32[]{:S(2)}) copy-start(bf16[4,2048,32]{1,2,0:T(8,128)(2,1)} %param.18) | copy-start | bytes 1572868
  12.3 14.3 %copy-start.18 = (s32[1,72]{1,0:T(1,128)S(1)}, s32[1,72]{1,0:T(1,128)}, u32[]{:S(2)}) copy-start(s32[1,72]{1,0:T(1,128)} %param.20) | copy-start | bytes 868
  12.3 14.5 %copy-start.15 = (s32[64,4]{0,1:T(4,128)S(1)}, s32[64,4]{0,1:T(4,128)}, u32[]{:S(2)}) copy-start(s32[64,4]{0,1:T(4,128)} %param.22) | copy-start | bytes 3076
  12.3 123.9 %all-to-all-start = ((bf16[3,32,32,256]{3,2,0,1:T(8,128)(2,1)}), bf16[3,32,32,256]{3,2,0,1:T(8,128)(2,1)}, u32[]{:S(2)}, u32[]{:S(2)}) async-start(bf16[3,32,32,256]{3,2,0,1:T(8,128)(2,1)} %copy.62), calls=%async_computation | async-start | bytes 3145728 | tf_op jit(solution)/shard_map/all_to_all | solution.py:111
  24.6 430.0 %all-gather.6.cloned.1.call-start = ((), (), s32[]{:S(2)}) async-start(), calls=%async_computation.6 | async-start | bytes 4325376 | tf_op jit(solution)/shard_map/all_gather | solution.py:174
  24.7 53.4 %collective-permute-start = (bf16[3,2048,32]{1,2,0:T(8,128)(2,1)S(1)}, bf16[3,2048,32]{1,2,0:T(8,128)(2,1)}, u32[]{:S(2)}, u32[]{:S(2)}) collective-permute-start(bf16[3,2048,32]{1,2,0:T(8,128)(2,1)S(1)} %slice.61), channel_id=1, source_target_pairs={{0,1},{1,0},{2,3},{3,2},{4,5},{5,4},{6,7},{7,6},{8,9},{9,8},{10,11... | collective-permute-start | bytes 1179656 | tf_op jit(solution)/shard_map/ppermute | solution.py:35
  27.1 105.9 %copy-start.8 = (s32[256]{0:T(256)}, s32[256]{0:T(256)S(1)}, u32[]{:S(2)}) copy-start(s32[256]{0:T(256)S(1)} %reshape.307) | copy-start | bytes 3076
  79.6 53.4 %collective-permute-start.1 = (bf16[3,2048,64]{1,2,0:T(8,128)(2,1)S(1)}, bf16[3,2048,64]{1,2,0:T(8,128)(2,1)}, u32[]{:S(2)}, u32[]{:S(2)}) collective-permute-start(bf16[3,2048,64]{1,2,0:T(8,128)(2,1)S(1)} %maximum_select_fusion.1), channel_id=1, source_target_pairs={{0,2},{1,3},{2,0},{3,1},{4,6},{5,7},{6,4},{7,5},{8,10},{9,11},{10,... | collective-permute-start | bytes 2359304 | tf_op jit(solution)/shard_map/ppermute | solution.py:35
  82.4 220.4 %copy-start.11 = (pred[8]{0:T(512)(128)(4,1)}, pred[8]{0:T(512)(128)(4,1)S(1)}, u32[]{:S(2)}) copy-start(pred[8]{0:T(512)(128)(4,1)S(1)} %iota_compare_fusion.9) | copy-start | bytes 28
  177.2 125.7 %copy-start.4 = (bf16[512,128]{0,1:T(8,128)(2,1)S(1)}, bf16[512,128]{0,1:T(8,128)(2,1)}, u32[]{:S(2)}) copy-start(bf16[512,128]{0,1:T(8,128)(2,1)} %get-tuple-element.120) | copy-start | bytes 393220
  187.2 115.6 %copy-start.14 = (pred[3584]{0:T(1024)(128)(4,1)}, pred[3584]{0:T(1024)(128)(4,1)S(1)}, u32[]{:S(2)}) copy-start(pred[3584]{0:T(1024)(128)(4,1)S(1)} %get-tuple-element.297) | copy-start | bytes 10756
  325.7 7.7 copy-start.12
  329.2 120.7 %all-to-all-start.1 = ((bf16[32,2,4096]{2,1,0:T(2,128)(2,1)}), bf16[32,2,4096]{2,1,0:T(2,128)(2,1)S(1)}, u32[]{:S(2)}, u32[]{:S(2)}) async-start(bf16[32,2,4096]{2,1,0:T(2,128)(2,1)} %reshape.323), calls=%async_computation.1 | async-start | bytes 1048576 | tf_op jit(solution)/shard_map/all_to_all | solution.py:163
  464.2 60.7 %collective-permute-start.2 = (bf16[8,1,5,2048]{3,2,1,0:T(8,128)(2,1)S(1)}, bf16[8,1,5,2048]{3,2,1,0:T(8,128)(2,1)S(1)}, u32[]{:S(2)}, u32[]{:S(2)}) collective-permute-start(bf16[8,1,5,2048]{3,2,1,0:T(8,128)(2,1)S(1)} %get-tuple-element.116), channel_id=1, source_target_pairs={{0,32},{32,0},{64,96},{96,64},{128,160},{160,128},{192,224},{224,1... | collective-permute-start | bytes 491528 | tf_op jit(solution)/shard_map/ppermute | solution.py:27
  519.9 7.9 collective-permute-start.3
  521.1 13.2 %collective-permute-start.4 = (bf16[8,1,5,2048]{3,2,1,0:T(8,128)(2,1)S(1)}, bf16[8,1,5,2048]{3,2,1,0:T(8,128)(2,1)S(1)}, u32[]{:S(2)}, u32[]{:S(2)}) collective-permute-start(bf16[8,1,5,2048]{3,2,1,0:T(8,128)(2,1)S(1)} %get-tuple-element.114), channel_id=1, source_target_pairs={{0,96},{32,64},{64,32},{96,0},{128,224},{160,192},{192,160},{224,1... | collective-permute-start | bytes 491528 | tf_op jit(solution)/shard_map/ppermute | solution.py:27
  521.6 19.5 %collective-permute-start.5 = (bf16[8,1,5,2048]{3,2,1,0:T(8,128)(2,1)S(1)}, bf16[8,1,5,2048]{3,2,1,0:T(8,128)(2,1)S(1)}, u32[]{:S(2)}, u32[]{:S(2)}) collective-permute-start(bf16[8,1,5,2048]{3,2,1,0:T(8,128)(2,1)S(1)} %get-tuple-element.113), channel_id=1, source_target_pairs={{0,128},{32,160},{64,192},{96,224},{128,0},{160,32},{192,64},{224,... | collective-permute-start | bytes 491528 | tf_op jit(solution)/shard_map/ppermute | solution.py:27
  524.3 22.7 %collective-permute-start.6 = (bf16[8,1,5,2048]{3,2,1,0:T(8,128)(2,1)S(1)}, bf16[8,1,5,2048]{3,2,1,0:T(8,128)(2,1)S(1)}, u32[]{:S(2)}, u32[]{:S(2)}) collective-permute-start(bf16[8,1,5,2048]{3,2,1,0:T(8,128)(2,1)S(1)} %get-tuple-element.112), channel_id=1, source_target_pairs={{0,160},{32,128},{64,224},{96,192},{128,32},{160,0},{192,96},{224,... | collective-permute-start | bytes 491528 | tf_op jit(solution)/shard_map/ppermute | solution.py:27
  524.9 22.1 %collective-permute-start.7 = (bf16[8,1,5,2048]{3,2,1,0:T(8,128)(2,1)S(1)}, bf16[8,1,5,2048]{3,2,1,0:T(8,128)(2,1)S(1)}, u32[]{:S(2)}, u32[]{:S(2)}) collective-permute-start(bf16[8,1,5,2048]{3,2,1,0:T(8,128)(2,1)S(1)} %get-tuple-element.111), channel_id=1, source_target_pairs={{0,192},{32,224},{64,128},{96,160},{128,64},{160,96},{192,0},{224,... | collective-permute-start | bytes 491528 | tf_op jit(solution)/shard_map/ppermute | solution.py:27
  527.8 23.3 %collective-permute-start.8 = (bf16[8,1,5,2048]{3,2,1,0:T(8,128)(2,1)S(1)}, bf16[8,1,5,2048]{3,2,1,0:T(8,128)(2,1)S(1)}, u32[]{:S(2)}, u32[]{:S(2)}) collective-permute-start(bf16[8,1,5,2048]{3,2,1,0:T(8,128)(2,1)S(1)} %get-tuple-element.110), channel_id=1, source_target_pairs={{0,224},{32,192},{64,160},{96,128},{128,96},{160,64},{192,32},{224... | collective-permute-start | bytes 491528 | tf_op jit(solution)/shard_map/ppermute | solution.py:27
  809.7 10.8 %copy-start.16 = (f32[64,4]{0,1:T(4,128)S(1)}, f32[64,4]{0,1:T(4,128)}, u32[]{:S(2)}) copy-start(f32[64,4]{0,1:T(4,128)} %param.23) | copy-start | bytes 3076
  811.5 26.9 %all-to-all-start.4 = ((bf16[8,8,5,2048]{3,0,2,1:T(8,128)(2,1)}), bf16[8,8,5,2048]{3,0,2,1:T(8,128)(2,1)S(1)}, u32[]{:S(2)}, u32[]{:S(2)}) async-start(bf16[8,8,5,2048]{3,0,2,1:T(8,128)(2,1)} %copy.74), calls=%async_computation.4 | async-start | bytes 2621440 | tf_op jit(solution)/shard_map/all_to_all | solution.py:217
  (15 other events, 45.4 us)
Sparse Core Ops, SparseCore 0:
  10.0 143.4 all-gather.3
  156.1 80.5 all-gather.5
